TPU v7x, 256 devices: a whole 4x4x8 slice. The times are simulated.
256 devices in a mesh: frames: 8 (over x, core), rows: 32 (over y, z).
Axes of the slice: x: 4, y: 4, z: 8, core: 2. Of those that a mesh axis runs over, the one named last changes fastest.
Arguments:
- observed: float32 [32, 2048, 2048], P('frames', 'rows'), may hold values from 0.25 to 4
- kernel: float32 [2048, 65], P('rows'), may hold values from 0.004 to 0.04
- row_shift: int32 [2048], P('rows'), may hold values from -8 to 8
- cycle_map: float32 [2048, 256], P('rows'), may hold values from 0 to 0.03125
- cycle_blocks: int32 [32, 8], P('rows'), may hold values from 0 to 63
- chi_map: bfloat16 [32, 2048, 720], P('rows'), may hold values from 0 to 3.0517578e-05
Outputs:
- binned: float32 [2048, 720], P('rows')
All inputs are finite; a program needn't handle non-finite values.
Results may differ from a plain program's by a relative error of at most 0.0003.
Values sent between devices are 32-bit elements; how exact they have to be, the bound alone decides.
A program may use at most 128 MiB of HBM per device.

v0:
```python
import jax
import jax.numpy as jnp
from jax import lax
from jax.sharding import PartitionSpec as P

SHIFT = 8
ITERS = 4
Q = 2048
CHI = 720
QB = 32
NB = 8


def shifted(block, axis, distance):
    devices = range(lax.axis_size(axis))
    route = [(i - distance, i) for i in devices if i - distance in devices]
    return lax.ppermute(block, axis, route)


def extended(cells, sides, width):
    for axis, dim in sides:
        count = lax.axis_size(axis)
        ends = count - 1
        head = lax.slice_in_dim(cells, 0, width, axis=dim)
        tail = lax.slice_in_dim(cells, cells.shape[dim] - width, cells.shape[dim], axis=dim)
        cells = jnp.concatenate(
            [
                lax.ppermute(tail, axis, [(i, (i + 1) % count) for i in range(ends)]),
                cells,
                lax.ppermute(head, axis, [((i + 1) % count, i) for i in range(ends)]),
            ],
            axis=dim,
        )
    return cells


def band_matrix(kernel, row_shift, first_row, total_rows, halo_rows):
    rows_here = kernel.shape[0]
    band_width = kernel.shape[1]
    half_band = (band_width - 1) // 2
    local_rows = jnp.arange(rows_here, dtype=jnp.int32)[:, None]
    tap_index = jnp.arange(band_width, dtype=jnp.int32)[None, :]
    target = local_rows + row_shift[:, None] + tap_index - half_band
    global_rows = target + first_row
    inside = (global_rows >= 0) & (global_rows < total_rows)
    weights = jnp.where(inside, kernel, jnp.float32(0.0))
    columns = jnp.arange(rows_here + 2 * halo_rows, dtype=jnp.int32)
    matches = (target[:, :, None] + halo_rows == columns[None, None, :]).astype(jnp.float32)
    return jnp.einsum("ik,ikj->ij", weights, matches, precision=lax.Precision.HIGHEST)


def rim_tables(rows_here, halo_rows):
    top_place = jnp.eye(halo_rows, rows_here, dtype=jnp.float32)
    bottom_place = jnp.eye(halo_rows, rows_here, k=rows_here - halo_rows, dtype=jnp.float32)
    return (top_place, bottom_place)


def body(observed, kernel, row_shift, cycle_map, cycle_blocks, chi_map):
    rows_here = observed.shape[1]
    tile_count = lax.axis_size("rows")
    first_row = lax.axis_index("rows") * rows_here
    halo_rows = (kernel.shape[1] - 1) // 2 + SHIFT
    band_mat = band_matrix(kernel, row_shift, first_row, rows_here * tile_count, halo_rows)
    top_place, bottom_place = rim_tables(rows_here, halo_rows)
    upper_band = band_mat[:, :halo_rows]
    centre_band = band_mat[:, halo_rows : halo_rows + rows_here]
    lower_band = band_mat[:, halo_rows + rows_here :]

    def spread(upper_rim, centre, lower_rim):
        from_below = shifted(upper_rim, "rows", -1)
        from_above = shifted(lower_rim, "rows", 1)
        centre = centre + jnp.einsum(
            "hr,fhc->frc", top_place, from_above, precision=lax.Precision.HIGHEST
        )
        return centre + jnp.einsum(
            "hr,fhc->frc", bottom_place, from_below, precision=lax.Precision.HIGHEST
        )

    norm_sums = spread(
        jnp.sum(upper_band, axis=0)[None, :, None],
        jnp.sum(centre_band, axis=0)[None, :, None],
        jnp.sum(lower_band, axis=0)[None, :, None],
    )
    estimate = observed
    for repeat in range(ITERS):
        padded = extended(estimate, (("rows", 1),), halo_rows)
        blurred = jnp.einsum("ij,fjc->fic", band_mat, padded, precision=lax.Precision.HIGHEST)
        ratios = observed / blurred
        upper_part = jnp.einsum("ij,fic->fjc", upper_band, ratios, precision=lax.Precision.HIGHEST)
        centre_part = jnp.einsum(
            "ij,fic->fjc", centre_band, ratios, precision=lax.Precision.HIGHEST
        )
        lower_part = jnp.einsum("ij,fic->fjc", lower_band, ratios, precision=lax.Precision.HIGHEST)
        backed = spread(upper_part, centre_part, lower_part)
        estimate = estimate * backed / norm_sums
    summed = jnp.sum(estimate, axis=0)
    cycle_part = jnp.einsum("rq,rc->qc", cycle_map, summed, precision=lax.Precision.HIGHEST).astype(
        jnp.bfloat16
    )
    blocks = jnp.dot(cycle_part, chi_map[0], preferred_element_type=jnp.float32).reshape(
        NB, QB, CHI
    )
    onehot = (jnp.arange(Q // QB, dtype=jnp.int32)[:, None] == cycle_blocks[0][None, :]).astype(
        jnp.float32
    )
    owned = lax.psum_scatter(
        jnp.einsum("kb,bqc->kqc", onehot, blocks, precision=lax.Precision.HIGHEST).reshape(Q, CHI),
        "rows",
        scatter_dimension=0,
        tiled=True,
    )
    binned = lax.psum(owned, "frames")
    return binned


def solution(mesh):
    return jax.shard_map(
        body,
        mesh=mesh,
        in_specs=(
            P("frames", "rows", None),
            P("rows", None),
            P("rows"),
            P("rows", None),
            P("rows", None),
            P("rows", None, None),
        ),
        out_specs=P("rows", None),
        check_vma=False,
    )
```

profile of v0, /device:TPU:8, one launch (start us, length us, event | category | flops | bytes accessed | tf_op | source)
XLA Modules:
  0.0 628.5 jit_solution(18317069830610186839)
XLA Ops:
  6.5 3.7 fusion.137
  10.2 3.8 collective-permute-start
  14.0 5.7 collective-permute-start.1
  20.0 2.2 fusion.24
  22.3 24.7 %collective-permute-done = f32[4,40,2048]{2,1,0:T(8,128)} collective-permute-done((f32[4,40,2048]{2,1,0:T(8,128)}, f32[4,40,2048]{2,1,0:T(8,128)}, u32[]{:S(2)}, u32[]{:S(2)}) %collective-permute-start) | collective-permute-done | bytes 1310752 | tf_op jit(solution)/shard_map/ppermute | solution.py:28
  48.1 6.2 fusion.52
  55.9 2.4 collective-permute-start.2
  59.8 6.0 collective-permute-start.3
  66.0 3.9 collective-permute-start.5
  69.9 2.1 collective-permute-start.4
  72.1 20.9 %collective-permute-done.5 = f32[1,40,1]{1,2,0:T(1,128)S(1)} collective-permute-done((f32[1,40,1]{1,2,0:T(1,128)S(1)}, f32[1,40,1]{1,2,0:T(1,128)S(1)}, u32[]{:S(2)}, u32[]{:S(2)}) %collective-permute-start.5) | collective-permute-done | bytes 192 | tf_op jit(solution)/shard_map/ppermute | solution.py:17
  93.4 2.1 fusion.83
  97.1 1.7 fusion.47
  99.1 4.0 collective-permute-start.6
  103.1 4.4 collective-permute-start.7
  107.5 25.0 %collective-permute-done.6 = f32[4,40,2048]{2,1,0:T(8,128)S(1)} collective-permute-done((f32[4,40,2048]{2,1,0:T(8,128)S(1)}, f32[4,40,2048]{2,1,0:T(8,128)S(1)}, u32[]{:S(2)}, u32[]{:S(2)}) %collective-permute-start.6) | collective-permute-done | bytes 1310752 | tf_op jit(solution)/shard_map/ppermute | solution.py:28
  133.7 3.1 fusion.55
  136.8 1.6 convolution_bitcast_fusion.5
  138.4 2.8 collective-permute-start.8
  142.7 5.9 collective-permute-start.9
  148.6 2.1 fusion.81
  150.7 20.2 %collective-permute-done.8 = f32[4,40,2048]{2,1,0:T(8,128)S(1)} collective-permute-done((f32[4,40,2048]{2,1,0:T(8,128)S(1)}, f32[4,40,2048]{2,1,0:T(8,128)S(1)}, u32[]{:S(2)}, u32[]{:S(2)}) %collective-permute-start.8) | collective-permute-done | bytes 1310752 | tf_op jit(solution)/shard_map/ppermute | solution.py:17
  173.6 1.7 fusion.48
  175.6 1.9 collective-permute-start.10
  177.5 6.5 %collective-permute-start.11 = (f32[4,40,2048]{2,1,0:T(8,128)S(1)}, f32[4,40,2048]{2,1,0:T(8,128)S(1)}, u32[]{:S(2)}, u32[]{:S(2)}) collective-permute-start(f32[4,40,2048]{2,1,0:T(8,128)S(1)} %get-tuple-element.10), channel_id=1, source_target_pairs={{1,0},{2,1},{3,2},{4,3},{5,4},{6,5},{7,6},{8,7},{9,8},{10,9},{11,1... | collective-permute-start | bytes 3932168 | tf_op jit(solution)/shard_map/ppermute | solution.py:30
  184.0 23.1 %collective-permute-done.10 = f32[4,40,2048]{2,1,0:T(8,128)S(1)} collective-permute-done((f32[4,40,2048]{2,1,0:T(8,128)S(1)}, f32[4,40,2048]{2,1,0:T(8,128)S(1)}, u32[]{:S(2)}, u32[]{:S(2)}) %collective-permute-start.10) | collective-permute-done | bytes 1310752 | tf_op jit(solution)/shard_map/ppermute | solution.py:28
  208.3 3.1 fusion.58
  211.4 1.6 convolution_bitcast_fusion.3
  213.0 1.9 collective-permute-start.12
  216.5 7.0 %collective-permute-start.13 = (f32[4,40,2048]{2,1,0:T(8,128)S(1)}, f32[4,40,2048]{2,1,0:T(8,128)S(1)}, u32[]{:S(2)}, u32[]{:S(2)}) collective-permute-start(f32[4,40,2048]{2,1,0:T(8,128)S(1)} %convolution_bitcast_fusion.2), channel_id=1, source_target_pairs={{1,0},{2,1},{3,2},{4,3},{5,4},{6,5},{7,6},{8,7},{9,8},{10,9},{11,1... | collective-permute-start | bytes 3932168 | tf_op jit(solution)/shard_map/ppermute | solution.py:17
  223.5 2.1 fusion.79
  225.5 18.1 %collective-permute-done.12 = f32[4,40,2048]{2,1,0:T(8,128)S(1)} collective-permute-done((f32[4,40,2048]{2,1,0:T(8,128)S(1)}, f32[4,40,2048]{2,1,0:T(8,128)S(1)}, u32[]{:S(2)}, u32[]{:S(2)}) %collective-permute-start.12) | collective-permute-done | bytes 1310752 | tf_op jit(solution)/shard_map/ppermute | solution.py:17
  246.4 1.7 fusion.49
  248.4 1.9 collective-permute-start.14
  250.3 6.5 %collective-permute-start.15 = (f32[4,40,2048]{2,1,0:T(8,128)S(1)}, f32[4,40,2048]{2,1,0:T(8,128)S(1)}, u32[]{:S(2)}, u32[]{:S(2)}) collective-permute-start(f32[4,40,2048]{2,1,0:T(8,128)S(1)} %get-tuple-element.8), channel_id=1, source_target_pairs={{1,0},{2,1},{3,2},{4,3},{5,4},{6,5},{7,6},{8,7},{9,8},{10,9},{11,1... | collective-permute-start | bytes 3932168 | tf_op jit(solution)/shard_map/ppermute | solution.py:30
  256.9 21.3 %collective-permute-done.14 = f32[4,40,2048]{2,1,0:T(8,128)S(1)} collective-permute-done((f32[4,40,2048]{2,1,0:T(8,128)S(1)}, f32[4,40,2048]{2,1,0:T(8,128)S(1)}, u32[]{:S(2)}, u32[]{:S(2)}) %collective-permute-start.14) | collective-permute-done | bytes 1310752 | tf_op jit(solution)/shard_map/ppermute | solution.py:28
  279.3 3.1 fusion.61
  284.0 1.9 collective-permute-start.16
  287.5 6.7 %collective-permute-start.17 = (f32[4,40,2048]{2,1,0:T(8,128)S(1)}, f32[4,40,2048]{2,1,0:T(8,128)S(1)}, u32[]{:S(2)}, u32[]{:S(2)}) collective-permute-start(f32[4,40,2048]{2,1,0:T(8,128)S(1)} %convolution_bitcast_fusion), channel_id=1, source_target_pairs={{1,0},{2,1},{3,2},{4,3},{5,4},{6,5},{7,6},{8,7},{9,8},{10,9},{11,1... | collective-permute-start | bytes 3932168 | tf_op jit(solution)/shard_map/ppermute | solution.py:17
  294.2 2.1 fusion.77
  296.2 16.5 %collective-permute-done.16 = f32[4,40,2048]{2,1,0:T(8,128)S(1)} collective-permute-done((f32[4,40,2048]{2,1,0:T(8,128)S(1)}, f32[4,40,2048]{2,1,0:T(8,128)S(1)}, u32[]{:S(2)}, u32[]{:S(2)}) %collective-permute-start.16) | collective-permute-done | bytes 1310752 | tf_op jit(solution)/shard_map/ppermute | solution.py:17
  315.5 1.7 fusion.64
  317.2 1.8 convolution_convert_fusion
  320.1 2.7 fusion.67
  322.8 6.3 %copy.21 = f32[64,32,720]{2,1,0:T(8,128)} copy(f32[64,32,720]{2,0,1:T(8,128)S(1)} %fusion.67) | data formatting | bytes 11796480 | tf_op jit(solution)/shard_map/kb,bqc->kqc/dot_general | solution.py:107
  329.2 224.2 %reduce-scatter.2.cloned.1.call-done = f32[64,720]{1,0:T(8,128)} async-done(((f32[2048,720]{1,0:T(8,128)}), f32[64,720]{1,0:T(8,128)}) %reduce-scatter.2.cloned.1.call-update) | async-done | bytes 184336 | tf_op jit(solution)/shard_map/reduce_scatter | solution.py:106
  553.5 66.4 %all-reduce.2.cloned.1.call-done = f32[64,720]{1,0:T(8,128)} async-done(((f32[64,720]{1,0:T(8,128)}), f32[64,720]{1,0:T(8,128)}) %all-reduce.2.cloned.1.call-update) | async-done | bytes 184336 | tf_op jit(solution)/shard_map/psum | solution.py:112
  619.8 1.6 copy.51
  (49 shorter events, 26.6 us)
Async XLA Ops:
  6.5 312.5 %copy-start = (bf16[1,2048,720]{1,2,0:T(8,128)(2,1)S(1)}, bf16[1,2048,720]{1,2,0:T(8,128)(2,1)}, u32[]{:S(2)}) copy-start(bf16[1,2048,720]{1,2,0:T(8,128)(2,1)} %param.11) | copy-start | bytes 8847364
  6.5 13.3 %copy-start.5 = (s32[64]{0:T(128)S(1)}, s32[64]{0:T(128)}, u32[]{:S(2)}) copy-start(s32[64]{0:T(128)} %param.8) | copy-start | bytes 772
  6.5 13.4 %copy-start.3 = (f32[64,65]{1,0:T(8,128)S(1)}, f32[64,65]{1,0:T(8,128)}, u32[]{:S(2)}) copy-start(f32[64,65]{1,0:T(8,128)} %param.7) | copy-start | bytes 49924
  6.5 546.9 %reduce-scatter.2.cloned.1.call-start = ((), (), s32[]{:S(2)}) async-start(), calls=%async_computation.1 | async-start | bytes 6488064 | tf_op jit(solution)/shard_map/reduce_scatter | solution.py:106
  10.2 36.7 %collective-permute-start = (f32[4,40,2048]{2,1,0:T(8,128)}, f32[4,40,2048]{2,1,0:T(8,128)}, u32[]{:S(2)}, u32[]{:S(2)}) collective-permute-start(f32[4,40,2048]{2,1,0:T(8,128)} %get-tuple-element.13), channel_id=1, source_target_pairs={{0,1},{1,2},{2,3},{3,4},{4,5},{5,6},{6,7},{7,8},{8,9},{9,10},{10,1... | collective-permute-start | bytes 3932168 | tf_op jit(solution)/shard_map/ppermute | solution.py:28
  14.0 34.1 %collective-permute-start.1 = (f32[4,40,2048]{2,1,0:T(8,128)}, f32[4,40,2048]{2,1,0:T(8,128)}, u32[]{:S(2)}, u32[]{:S(2)}) collective-permute-start(f32[4,40,2048]{2,1,0:T(8,128)} %get-tuple-element.14), channel_id=1, source_target_pairs={{1,0},{2,1},{3,2},{4,3},{5,4},{6,5},{7,6},{8,7},{9,8},{10,9},{11,1... | collective-permute-start | bytes 3932168 | tf_op jit(solution)/shard_map/ppermute | solution.py:30
  55.9 39.6 %collective-permute-start.2 = (f32[4,40,2048]{2,1,0:T(8,128)S(1)}, f32[4,40,2048]{2,1,0:T(8,128)S(1)}, u32[]{:S(2)}, u32[]{:S(2)}) collective-permute-start(f32[4,40,2048]{2,1,0:T(8,128)S(1)} %convolution_bitcast_fusion.7), channel_id=1, source_target_pairs={{0,1},{1,2},{2,3},{3,4},{4,5},{5,6},{6,7},{7,8},{8,9},{9,10},{10,1... | collective-permute-start | bytes 3932168 | tf_op jit(solution)/shard_map/ppermute | solution.py:17
  59.8 37.0 %collective-permute-start.3 = (f32[4,40,2048]{2,1,0:T(8,128)S(1)}, f32[4,40,2048]{2,1,0:T(8,128)S(1)}, u32[]{:S(2)}, u32[]{:S(2)}) collective-permute-start(f32[4,40,2048]{2,1,0:T(8,128)S(1)} %convolution_bitcast_fusion.6), channel_id=1, source_target_pairs={{1,0},{2,1},{3,2},{4,3},{5,4},{6,5},{7,6},{8,7},{9,8},{10,9},{11,1... | collective-permute-start | bytes 3932168 | tf_op jit(solution)/shard_map/ppermute | solution.py:17
  66.0 27.1 %collective-permute-start.5 = (f32[1,40,1]{1,2,0:T(1,128)S(1)}, f32[1,40,1]{1,2,0:T(1,128)S(1)}, u32[]{:S(2)}, u32[]{:S(2)}) collective-permute-start(f32[1,40,1]{1,2,0:T(1,128)S(1)} %bitcast.192), channel_id=1, source_target_pairs={{1,0},{2,1},{3,2},{4,3},{5,4},{6,5},{7,6},{8,7},{9,8},{10,9},{11,1... | collective-permute-start | bytes 488 | tf_op jit(solution)/shard_map/ppermute | solution.py:17
  69.9 23.3 %collective-permute-start.4 = (f32[1,40,1]{1,2,0:T(1,128)S(1)}, f32[1,40,1]{1,2,0:T(1,128)S(1)}, u32[]{:S(2)}, u32[]{:S(2)}) collective-permute-start(f32[1,40,1]{1,2,0:T(1,128)S(1)} %bitcast.191), channel_id=1, source_target_pairs={{0,1},{1,2},{2,3},{3,4},{4,5},{5,6},{6,7},{7,8},{8,9},{9,10},{10,1... | collective-permute-start | bytes 488 | tf_op jit(solution)/shard_map/ppermute | solution.py:17
  95.5 1.6 copy-start.1
  99.1 33.4 %collective-permute-start.6 = (f32[4,40,2048]{2,1,0:T(8,128)S(1)}, f32[4,40,2048]{2,1,0:T(8,128)S(1)}, u32[]{:S(2)}, u32[]{:S(2)}) collective-permute-start(f32[4,40,2048]{2,1,0:T(8,128)S(1)} %get-tuple-element.11), channel_id=1, source_target_pairs={{0,1},{1,2},{2,3},{3,4},{4,5},{5,6},{6,7},{7,8},{8,9},{9,10},{10,1... | collective-permute-start | bytes 3932168 | tf_op jit(solution)/shard_map/ppermute | solution.py:28
  103.1 30.6 %collective-permute-start.7 = (f32[4,40,2048]{2,1,0:T(8,128)S(1)}, f32[4,40,2048]{2,1,0:T(8,128)S(1)}, u32[]{:S(2)}, u32[]{:S(2)}) collective-permute-start(f32[4,40,2048]{2,1,0:T(8,128)S(1)} %get-tuple-element.12), channel_id=1, source_target_pairs={{1,0},{2,1},{3,2},{4,3},{5,4},{6,5},{7,6},{8,7},{9,8},{10,9},{11,1... | collective-permute-start | bytes 3932168 | tf_op jit(solution)/shard_map/ppermute | solution.py:30
  138.4 32.5 %collective-permute-start.8 = (f32[4,40,2048]{2,1,0:T(8,128)S(1)}, f32[4,40,2048]{2,1,0:T(8,128)S(1)}, u32[]{:S(2)}, u32[]{:S(2)}) collective-permute-start(f32[4,40,2048]{2,1,0:T(8,128)S(1)} %convolution_bitcast_fusion.5), channel_id=1, source_target_pairs={{0,1},{1,2},{2,3},{3,4},{4,5},{5,6},{6,7},{7,8},{8,9},{9,10},{10,1... | collective-permute-start | bytes 3932168 | tf_op jit(solution)/shard_map/ppermute | solution.py:17
  142.7 30.9 %collective-permute-start.9 = (f32[4,40,2048]{2,1,0:T(8,128)S(1)}, f32[4,40,2048]{2,1,0:T(8,128)S(1)}, u32[]{:S(2)}, u32[]{:S(2)}) collective-permute-start(f32[4,40,2048]{2,1,0:T(8,128)S(1)} %convolution_bitcast_fusion.4), channel_id=1, source_target_pairs={{1,0},{2,1},{3,2},{4,3},{5,4},{6,5},{7,6},{8,7},{9,8},{10,9},{11,1... | collective-permute-start | bytes 3932168 | tf_op jit(solution)/shard_map/ppermute | solution.py:17
  175.6 31.6 %collective-permute-start.10 = (f32[4,40,2048]{2,1,0:T(8,128)S(1)}, f32[4,40,2048]{2,1,0:T(8,128)S(1)}, u32[]{:S(2)}, u32[]{:S(2)}) collective-permute-start(f32[4,40,2048]{2,1,0:T(8,128)S(1)} %get-tuple-element.9), channel_id=1, source_target_pairs={{0,1},{1,2},{2,3},{3,4},{4,5},{5,6},{6,7},{7,8},{8,9},{9,10},{10,1... | collective-permute-start | bytes 3932168 | tf_op jit(solution)/shard_map/ppermute | solution.py:28
  177.5 30.8 %collective-permute-start.11 = (f32[4,40,2048]{2,1,0:T(8,128)S(1)}, f32[4,40,2048]{2,1,0:T(8,128)S(1)}, u32[]{:S(2)}, u32[]{:S(2)}) collective-permute-start(f32[4,40,2048]{2,1,0:T(8,128)S(1)} %get-tuple-element.10), channel_id=1, source_target_pairs={{1,0},{2,1},{3,2},{4,3},{5,4},{6,5},{7,6},{8,7},{9,8},{10,9},{11,1... | collective-permute-start | bytes 3932168 | tf_op jit(solution)/shard_map/ppermute | solution.py:30
  213.0 30.6 %collective-permute-start.12 = (f32[4,40,2048]{2,1,0:T(8,128)S(1)}, f32[4,40,2048]{2,1,0:T(8,128)S(1)}, u32[]{:S(2)}, u32[]{:S(2)}) collective-permute-start(f32[4,40,2048]{2,1,0:T(8,128)S(1)} %convolution_bitcast_fusion.3), channel_id=1, source_target_pairs={{0,1},{1,2},{2,3},{3,4},{4,5},{5,6},{6,7},{7,8},{8,9},{9,10},{10,1... | collective-permute-start | bytes 3932168 | tf_op jit(solution)/shard_map/ppermute | solution.py:17
  216.5 29.9 %collective-permute-start.13 = (f32[4,40,2048]{2,1,0:T(8,128)S(1)}, f32[4,40,2048]{2,1,0:T(8,128)S(1)}, u32[]{:S(2)}, u32[]{:S(2)}) collective-permute-start(f32[4,40,2048]{2,1,0:T(8,128)S(1)} %convolution_bitcast_fusion.2), channel_id=1, source_target_pairs={{1,0},{2,1},{3,2},{4,3},{5,4},{6,5},{7,6},{8,7},{9,8},{10,9},{11,1... | collective-permute-start | bytes 3932168 | tf_op jit(solution)/shard_map/ppermute | solution.py:17
  248.4 29.7 %collective-permute-start.14 = (f32[4,40,2048]{2,1,0:T(8,128)S(1)}, f32[4,40,2048]{2,1,0:T(8,128)S(1)}, u32[]{:S(2)}, u32[]{:S(2)}) collective-permute-start(f32[4,40,2048]{2,1,0:T(8,128)S(1)} %get-tuple-element.7), channel_id=1, source_target_pairs={{0,1},{1,2},{2,3},{3,4},{4,5},{5,6},{6,7},{7,8},{8,9},{9,10},{10,1... | collective-permute-start | bytes 3932168 | tf_op jit(solution)/shard_map/ppermute | solution.py:28
  250.3 29.0 %collective-permute-start.15 = (f32[4,40,2048]{2,1,0:T(8,128)S(1)}, f32[4,40,2048]{2,1,0:T(8,128)S(1)}, u32[]{:S(2)}, u32[]{:S(2)}) collective-permute-start(f32[4,40,2048]{2,1,0:T(8,128)S(1)} %get-tuple-element.8), channel_id=1, source_target_pairs={{1,0},{2,1},{3,2},{4,3},{5,4},{6,5},{7,6},{8,7},{9,8},{10,9},{11,1... | collective-permute-start | bytes 3932168 | tf_op jit(solution)/shard_map/ppermute | solution.py:30
  284.0 28.8 %collective-permute-start.16 = (f32[4,40,2048]{2,1,0:T(8,128)S(1)}, f32[4,40,2048]{2,1,0:T(8,128)S(1)}, u32[]{:S(2)}, u32[]{:S(2)}) collective-permute-start(f32[4,40,2048]{2,1,0:T(8,128)S(1)} %convolution_bitcast_fusion.1), channel_id=1, source_target_pairs={{0,1},{1,2},{2,3},{3,4},{4,5},{5,6},{6,7},{7,8},{8,9},{9,10},{10,1... | collective-permute-start | bytes 3932168 | tf_op jit(solution)/shard_map/ppermute | solution.py:17
  287.5 28.0 %collective-permute-start.17 = (f32[4,40,2048]{2,1,0:T(8,128)S(1)}, f32[4,40,2048]{2,1,0:T(8,128)S(1)}, u32[]{:S(2)}, u32[]{:S(2)}) collective-permute-start(f32[4,40,2048]{2,1,0:T(8,128)S(1)} %convolution_bitcast_fusion), channel_id=1, source_target_pairs={{1,0},{2,1},{3,2},{4,3},{5,4},{6,5},{7,6},{8,7},{9,8},{10,9},{11,1... | collective-permute-start | bytes 3932168 | tf_op jit(solution)/shard_map/ppermute | solution.py:17
  314.1 3.1 copy-start.2
  319.1 1.0 copy-start.4
  329.2 290.7 %all-reduce.2.cloned.1.call-start = ((), (), s32[]{:S(2)}) async-start(), calls=%async_computation.2 | async-start | bytes 393216 | tf_op jit(solution)/shard_map/psum | solution.py:112
Sparse Core Ops, SparseCore 0:
  329.3 224.1 reduce-scatter.1
  555.9 63.9 all-reduce.1
where the time goes:
time: 635 us; the launch traced here: 628 us
  waiting for transfers between devices  470 us (74%)
  starting transfers between devices  75.4 us (12%)
  matrix products  56.2 us (9%)
  between operations  14.1 us (2%)
  local copies, waits for them, and re-layouts  12.8 us (2%)
    reduce_scatter x1, waiting for transfers between devices, body(): lax.psum_scatter(jnp.einsum('kb,bqc->kqc', onehot, blocks, precision=lax....  224 us
    ppermute x4, waiting for transfers between devices, extended(): lax.ppermute(tail, axis, [(i, (i + 1) % count) for i in range(ends)])  94.1 us
    ppermute x10, waiting for transfers between devices, shifted(): return lax.ppermute(block, axis, route)  80.2 us
    psum x1, waiting for transfers between devices, body(): binned = lax.psum(owned, 'frames')  66.4 us
    ppermute x10, starting transfers between devices, shifted(): return lax.ppermute(block, axis, route)  40.5 us
    ppermute x4, starting transfers between devices, extended(): lax.ppermute(head, axis, [((i + 1) % count, i) for i in range(ends)])  23.2 us
    dot_general x4, matrix products, body(): jnp.einsum('ij,fjc->fic', band_mat, padded, precision=lax.Precision.HIGHEST)  15.4 us
  transfers between devices with their start and end apart: 20, of which 17 were waited for; matrix products, arithmetic and copies ran while one was open for 4% of the time, Pallas kernels for 0%

commit v1 on v0

--- a/solution.py
+++ b/solution.py
@@ -109,7 +109,7 @@
         scatter_dimension=0,
         tiled=True,
     )
-    binned = lax.psum(owned, "frames")
+    binned = jnp.sum(lax.all_gather(owned, "frames"), axis=0)
     return binned
 
 

time: 635 us -> 598 us (0.942)
  waiting for transfers between devices: 470 us -> 431 us
    psum x1 -> x0, waiting for transfers between devices: 66.4 us -> none  [body(): binned = lax.psum(owned, 'frames')]
    all_gather x0 -> x1, waiting for transfers between devices: none -> 28.1 us  [body(): binned = jnp.sum(lax.all_gather(owned, 'frames'), axis=0)]
where the time goes in v1:
time: 598 us; the launch traced here: 591 us
  waiting for transfers between devices  431 us (72%)
  starting transfers between devices  75.4 us (13%)
  matrix products  56.1 us (9%)
  between operations  14.1 us (2%)
  local copies, waits for them, and re-layouts  11.2 us (2%)
    reduce_scatter x1, waiting for transfers between devices, body(): lax.psum_scatter(jnp.einsum('kb,bqc->kqc', onehot, blocks, precision=lax....  224 us
    ppermute x4, waiting for transfers between devices, extended(): lax.ppermute(tail, axis, [(i, (i + 1) % count) for i in range(ends)])  94.1 us
    ppermute x10, waiting for transfers between devices, shifted(): return lax.ppermute(block, axis, route)  80.2 us
    ppermute x10, starting transfers between devices, shifted(): return lax.ppermute(block, axis, route)  40.5 us
    all_gather x1, waiting for transfers between devices, body(): binned = jnp.sum(lax.all_gather(owned, 'frames'), axis=0)  28.1 us
    ppermute x4, starting transfers between devices, extended(): lax.ppermute(head, axis, [((i + 1) % count, i) for i in range(ends)])  23.2 us
    dot_general x4, matrix products, body(): jnp.einsum('ij,fjc->fic', band_mat, padded, precision=lax.Precision.HIGHEST)  15.4 us
  transfers between devices with their start and end apart: 20, of which 17 were waited for; matrix products, arithmetic and copies ran while one was open for 4% of the time, Pallas kernels for 0%

profile of v1, /device:TPU:8, one launch (start us, length us, event | category | flops | bytes accessed | tf_op | source)
XLA Modules:
  0.0 590.8 jit_solution(14735502097046653515)
XLA Ops:
  6.5 3.7 fusion.137
  10.2 3.8 collective-permute-start
  14.0 5.7 collective-permute-start.1
  20.0 2.2 fusion.24
  22.3 24.7 %collective-permute-done = f32[4,40,2048]{2,1,0:T(8,128)} collective-permute-done((f32[4,40,2048]{2,1,0:T(8,128)}, f32[4,40,2048]{2,1,0:T(8,128)}, u32[]{:S(2)}, u32[]{:S(2)}) %collective-permute-start) | collective-permute-done | bytes 1310752 | tf_op jit(solution)/shard_map/ppermute | solution.py:28
  48.1 6.2 %fusion.52 = f32[4,64,2048]{2,1,0:T(8,128)S(1)} fusion(f32[4,64,2048]{2,1,0:T(8,128)} %param.6, f32[4,40,2048]{2,1,0:T(8,128)} %collective-permute-done.1, f32[4,40,2048]{2,1,0:T(8,128)} %collective-permute-done, f32[64,1,144]{2,1,0:T(1,128)S(1)} %fusion.24), kind=kOutput, calls=%fused_computation.62 | convolution fusion | flops 908853248 | bytes 6852608 | tf_op jit(solution)/shard_map/ij,fjc->fic/dot_general | solution.py:87
  55.9 2.4 collective-permute-start.2
  59.8 6.0 %collective-permute-start.3 = (f32[4,40,2048]{2,1,0:T(8,128)S(1)}, f32[4,40,2048]{2,1,0:T(8,128)S(1)}, u32[]{:S(2)}, u32[]{:S(2)}) collective-permute-start(f32[4,40,2048]{2,1,0:T(8,128)S(1)} %convolution_bitcast_fusion.6), channel_id=1, source_target_pairs={{1,0},{2,1},{3,2},{4,3},{5,4},{6,5},{7,6},{8,7},{9,8},{10,9},{11,1... | collective-permute-start | bytes 3932168 | tf_op jit(solution)/shard_map/ppermute | solution.py:17
  66.0 3.9 collective-permute-start.5
  69.9 2.1 collective-permute-start.4
  72.1 20.9 %collective-permute-done.5 = f32[1,40,1]{1,2,0:T(1,128)S(1)} collective-permute-done((f32[1,40,1]{1,2,0:T(1,128)S(1)}, f32[1,40,1]{1,2,0:T(1,128)S(1)}, u32[]{:S(2)}, u32[]{:S(2)}) %collective-permute-start.5) | collective-permute-done | bytes 192 | tf_op jit(solution)/shard_map/ppermute | solution.py:17
  93.4 2.1 fusion.83
  97.1 1.7 fusion.47
  99.1 4.0 collective-permute-start.6
  103.1 4.4 collective-permute-start.7
  107.5 25.0 %collective-permute-done.6 = f32[4,40,2048]{2,1,0:T(8,128)S(1)} collective-permute-done((f32[4,40,2048]{2,1,0:T(8,128)S(1)}, f32[4,40,2048]{2,1,0:T(8,128)S(1)}, u32[]{:S(2)}, u32[]{:S(2)}) %collective-permute-start.6) | collective-permute-done | bytes 1310752 | tf_op jit(solution)/shard_map/ppermute | solution.py:28
  133.7 3.1 fusion.55
  136.8 1.6 convolution_bitcast_fusion.5
  138.4 2.8 collective-permute-start.8
  142.7 5.9 collective-permute-start.9
  148.6 2.1 fusion.81
  150.7 20.2 %collective-permute-done.8 = f32[4,40,2048]{2,1,0:T(8,128)S(1)} collective-permute-done((f32[4,40,2048]{2,1,0:T(8,128)S(1)}, f32[4,40,2048]{2,1,0:T(8,128)S(1)}, u32[]{:S(2)}, u32[]{:S(2)}) %collective-permute-start.8) | collective-permute-done | bytes 1310752 | tf_op jit(solution)/shard_map/ppermute | solution.py:17
  173.6 1.7 fusion.48
  175.6 1.9 collective-permute-start.10
  177.5 6.5 %collective-permute-start.11 = (f32[4,40,2048]{2,1,0:T(8,128)S(1)}, f32[4,40,2048]{2,1,0:T(8,128)S(1)}, u32[]{:S(2)}, u32[]{:S(2)}) collective-permute-start(f32[4,40,2048]{2,1,0:T(8,128)S(1)} %get-tuple-element.10), channel_id=1, source_target_pairs={{1,0},{2,1},{3,2},{4,3},{5,4},{6,5},{7,6},{8,7},{9,8},{10,9},{11,1... | collective-permute-start | bytes 3932168 | tf_op jit(solution)/shard_map/ppermute | solution.py:30
  184.0 23.1 %collective-permute-done.10 = f32[4,40,2048]{2,1,0:T(8,128)S(1)} collective-permute-done((f32[4,40,2048]{2,1,0:T(8,128)S(1)}, f32[4,40,2048]{2,1,0:T(8,128)S(1)}, u32[]{:S(2)}, u32[]{:S(2)}) %collective-permute-start.10) | collective-permute-done | bytes 1310752 | tf_op jit(solution)/shard_map/ppermute | solution.py:28
  208.3 3.1 fusion.58
  211.4 1.6 convolution_bitcast_fusion.3
  213.0 1.9 collective-permute-start.12
  216.5 7.0 %collective-permute-start.13 = (f32[4,40,2048]{2,1,0:T(8,128)S(1)}, f32[4,40,2048]{2,1,0:T(8,128)S(1)}, u32[]{:S(2)}, u32[]{:S(2)}) collective-permute-start(f32[4,40,2048]{2,1,0:T(8,128)S(1)} %convolution_bitcast_fusion.2), channel_id=1, source_target_pairs={{1,0},{2,1},{3,2},{4,3},{5,4},{6,5},{7,6},{8,7},{9,8},{10,9},{11,1... | collective-permute-start | bytes 3932168 | tf_op jit(solution)/shard_map/ppermute | solution.py:17
  223.5 2.1 fusion.79
  225.5 18.1 %collective-permute-done.12 = f32[4,40,2048]{2,1,0:T(8,128)S(1)} collective-permute-done((f32[4,40,2048]{2,1,0:T(8,128)S(1)}, f32[4,40,2048]{2,1,0:T(8,128)S(1)}, u32[]{:S(2)}, u32[]{:S(2)}) %collective-permute-start.12) | collective-permute-done | bytes 1310752 | tf_op jit(solution)/shard_map/ppermute | solution.py:17
  246.4 1.7 fusion.49
  248.4 1.9 collective-permute-start.14
  250.3 6.5 %collective-permute-start.15 = (f32[4,40,2048]{2,1,0:T(8,128)S(1)}, f32[4,40,2048]{2,1,0:T(8,128)S(1)}, u32[]{:S(2)}, u32[]{:S(2)}) collective-permute-start(f32[4,40,2048]{2,1,0:T(8,128)S(1)} %get-tuple-element.8), channel_id=1, source_target_pairs={{1,0},{2,1},{3,2},{4,3},{5,4},{6,5},{7,6},{8,7},{9,8},{10,9},{11,1... | collective-permute-start | bytes 3932168 | tf_op jit(solution)/shard_map/ppermute | solution.py:30
  256.9 21.3 %collective-permute-done.14 = f32[4,40,2048]{2,1,0:T(8,128)S(1)} collective-permute-done((f32[4,40,2048]{2,1,0:T(8,128)S(1)}, f32[4,40,2048]{2,1,0:T(8,128)S(1)}, u32[]{:S(2)}, u32[]{:S(2)}) %collective-permute-start.14) | collective-permute-done | bytes 1310752 | tf_op jit(solution)/shard_map/ppermute | solution.py:28
  279.3 3.1 fusion.61
  284.0 1.9 collective-permute-start.16
  287.5 6.7 %collective-permute-start.17 = (f32[4,40,2048]{2,1,0:T(8,128)S(1)}, f32[4,40,2048]{2,1,0:T(8,128)S(1)}, u32[]{:S(2)}, u32[]{:S(2)}) collective-permute-start(f32[4,40,2048]{2,1,0:T(8,128)S(1)} %convolution_bitcast_fusion), channel_id=1, source_target_pairs={{1,0},{2,1},{3,2},{4,3},{5,4},{6,5},{7,6},{8,7},{9,8},{10,9},{11,1... | collective-permute-start | bytes 3932168 | tf_op jit(solution)/shard_map/ppermute | solution.py:17
  294.2 2.1 fusion.77
  296.2 16.5 %collective-permute-done.16 = f32[4,40,2048]{2,1,0:T(8,128)S(1)} collective-permute-done((f32[4,40,2048]{2,1,0:T(8,128)S(1)}, f32[4,40,2048]{2,1,0:T(8,128)S(1)}, u32[]{:S(2)}, u32[]{:S(2)}) %collective-permute-start.16) | collective-permute-done | bytes 1310752 | tf_op jit(solution)/shard_map/ppermute | solution.py:17
  315.5 1.6 fusion.64
  317.1 1.8 convolution_convert_fusion
  320.0 2.7 fusion.67
  322.8 6.3 %copy.21 = f32[64,32,720]{2,1,0:T(8,128)} copy(f32[64,32,720]{2,0,1:T(8,128)S(1)} %fusion.67) | data formatting | bytes 11796480 | tf_op jit(solution)/shard_map/kb,bqc->kqc/dot_general | solution.py:107
  329.2 224.3 %reduce-scatter.2.cloned.1.call-done = f32[64,720]{1,0:T(8,128)} async-done(((f32[2048,720]{1,0:T(8,128)}), f32[64,720]{1,0:T(8,128)}) %reduce-scatter.2.cloned.1.call-update) | async-done | bytes 184336 | tf_op jit(solution)/shard_map/reduce_scatter | solution.py:106
  553.5 28.1 %all-gather.3.cloned.1.call-done = f32[512,720]{1,0:T(8,128)} async-done(((f32[64,720]{1,0:T(8,128)}), f32[512,720]{1,0:T(8,128)}) %all-gather.3.cloned.1.call-update) | async-done | bytes 1474576 | tf_op jit(solution)/shard_map/all_gather | solution.py:112
  581.6 2.2 reduce_sum.49
  (49 shorter events, 26.6 us)
Async XLA Ops:
  6.5 312.5 %copy-start = (bf16[1,2048,720]{1,2,0:T(8,128)(2,1)S(1)}, bf16[1,2048,720]{1,2,0:T(8,128)(2,1)}, u32[]{:S(2)}) copy-start(bf16[1,2048,720]{1,2,0:T(8,128)(2,1)} %param.11) | copy-start | bytes 8847364
  6.5 13.3 %copy-start.5 = (s32[64]{0:T(128)S(1)}, s32[64]{0:T(128)}, u32[]{:S(2)}) copy-start(s32[64]{0:T(128)} %param.8) | copy-start | bytes 772
  6.5 13.4 %copy-start.3 = (f32[64,65]{1,0:T(8,128)S(1)}, f32[64,65]{1,0:T(8,128)}, u32[]{:S(2)}) copy-start(f32[64,65]{1,0:T(8,128)} %param.7) | copy-start | bytes 49924
  6.5 546.9 %reduce-scatter.2.cloned.1.call-start = ((), (), s32[]{:S(2)}) async-start(), calls=%async_computation.1 | async-start | bytes 6488064 | tf_op jit(solution)/shard_map/reduce_scatter | solution.py:106
  10.2 36.7 %collective-permute-start = (f32[4,40,2048]{2,1,0:T(8,128)}, f32[4,40,2048]{2,1,0:T(8,128)}, u32[]{:S(2)}, u32[]{:S(2)}) collective-permute-start(f32[4,40,2048]{2,1,0:T(8,128)} %get-tuple-element.13), channel_id=1, source_target_pairs={{0,1},{1,2},{2,3},{3,4},{4,5},{5,6},{6,7},{7,8},{8,9},{9,10},{10,1... | collective-permute-start | bytes 3932168 | tf_op jit(solution)/shard_map/ppermute | solution.py:28
  14.0 34.1 %collective-permute-start.1 = (f32[4,40,2048]{2,1,0:T(8,128)}, f32[4,40,2048]{2,1,0:T(8,128)}, u32[]{:S(2)}, u32[]{:S(2)}) collective-permute-start(f32[4,40,2048]{2,1,0:T(8,128)} %get-tuple-element.14), channel_id=1, source_target_pairs={{1,0},{2,1},{3,2},{4,3},{5,4},{6,5},{7,6},{8,7},{9,8},{10,9},{11,1... | collective-permute-start | bytes 3932168 | tf_op jit(solution)/shard_map/ppermute | solution.py:30
  55.9 39.6 %collective-permute-start.2 = (f32[4,40,2048]{2,1,0:T(8,128)S(1)}, f32[4,40,2048]{2,1,0:T(8,128)S(1)}, u32[]{:S(2)}, u32[]{:S(2)}) collective-permute-start(f32[4,40,2048]{2,1,0:T(8,128)S(1)} %convolution_bitcast_fusion.7), channel_id=1, source_target_pairs={{0,1},{1,2},{2,3},{3,4},{4,5},{5,6},{6,7},{7,8},{8,9},{9,10},{10,1... | collective-permute-start | bytes 3932168 | tf_op jit(solution)/shard_map/ppermute | solution.py:17
  59.8 37.0 %collective-permute-start.3 = (f32[4,40,2048]{2,1,0:T(8,128)S(1)}, f32[4,40,2048]{2,1,0:T(8,128)S(1)}, u32[]{:S(2)}, u32[]{:S(2)}) collective-permute-start(f32[4,40,2048]{2,1,0:T(8,128)S(1)} %convolution_bitcast_fusion.6), channel_id=1, source_target_pairs={{1,0},{2,1},{3,2},{4,3},{5,4},{6,5},{7,6},{8,7},{9,8},{10,9},{11,1... | collective-permute-start | bytes 3932168 | tf_op jit(solution)/shard_map/ppermute | solution.py:17
  66.0 27.1 %collective-permute-start.5 = (f32[1,40,1]{1,2,0:T(1,128)S(1)}, f32[1,40,1]{1,2,0:T(1,128)S(1)}, u32[]{:S(2)}, u32[]{:S(2)}) collective-permute-start(f32[1,40,1]{1,2,0:T(1,128)S(1)} %bitcast.194), channel_id=1, source_target_pairs={{1,0},{2,1},{3,2},{4,3},{5,4},{6,5},{7,6},{8,7},{9,8},{10,9},{11,1... | collective-permute-start | bytes 488 | tf_op jit(solution)/shard_map/ppermute | solution.py:17
  69.9 23.3 %collective-permute-start.4 = (f32[1,40,1]{1,2,0:T(1,128)S(1)}, f32[1,40,1]{1,2,0:T(1,128)S(1)}, u32[]{:S(2)}, u32[]{:S(2)}) collective-permute-start(f32[1,40,1]{1,2,0:T(1,128)S(1)} %bitcast.193), channel_id=1, source_target_pairs={{0,1},{1,2},{2,3},{3,4},{4,5},{5,6},{6,7},{7,8},{8,9},{9,10},{10,1... | collective-permute-start | bytes 488 | tf_op jit(solution)/shard_map/ppermute | solution.py:17
  95.5 1.6 copy-start.1
  99.1 33.4 %collective-permute-start.6 = (f32[4,40,2048]{2,1,0:T(8,128)S(1)}, f32[4,40,2048]{2,1,0:T(8,128)S(1)}, u32[]{:S(2)}, u32[]{:S(2)}) collective-permute-start(f32[4,40,2048]{2,1,0:T(8,128)S(1)} %get-tuple-element.11), channel_id=1, source_target_pairs={{0,1},{1,2},{2,3},{3,4},{4,5},{5,6},{6,7},{7,8},{8,9},{9,10},{10,1... | collective-permute-start | bytes 3932168 | tf_op jit(solution)/shard_map/ppermute | solution.py:28
  103.1 30.6 %collective-permute-start.7 = (f32[4,40,2048]{2,1,0:T(8,128)S(1)}, f32[4,40,2048]{2,1,0:T(8,128)S(1)}, u32[]{:S(2)}, u32[]{:S(2)}) collective-permute-start(f32[4,40,2048]{2,1,0:T(8,128)S(1)} %get-tuple-element.12), channel_id=1, source_target_pairs={{1,0},{2,1},{3,2},{4,3},{5,4},{6,5},{7,6},{8,7},{9,8},{10,9},{11,1... | collective-permute-start | bytes 3932168 | tf_op jit(solution)/shard_map/ppermute | solution.py:30
  138.4 32.5 %collective-permute-start.8 = (f32[4,40,2048]{2,1,0:T(8,128)S(1)}, f32[4,40,2048]{2,1,0:T(8,128)S(1)}, u32[]{:S(2)}, u32[]{:S(2)}) collective-permute-start(f32[4,40,2048]{2,1,0:T(8,128)S(1)} %convolution_bitcast_fusion.5), channel_id=1, source_target_pairs={{0,1},{1,2},{2,3},{3,4},{4,5},{5,6},{6,7},{7,8},{8,9},{9,10},{10,1... | collective-permute-start | bytes 3932168 | tf_op jit(solution)/shard_map/ppermute | solution.py:17
  142.7 30.9 %collective-permute-start.9 = (f32[4,40,2048]{2,1,0:T(8,128)S(1)}, f32[4,40,2048]{2,1,0:T(8,128)S(1)}, u32[]{:S(2)}, u32[]{:S(2)}) collective-permute-start(f32[4,40,2048]{2,1,0:T(8,128)S(1)} %convolution_bitcast_fusion.4), channel_id=1, source_target_pairs={{1,0},{2,1},{3,2},{4,3},{5,4},{6,5},{7,6},{8,7},{9,8},{10,9},{11,1... | collective-permute-start | bytes 3932168 | tf_op jit(solution)/shard_map/ppermute | solution.py:17
  175.6 31.6 %collective-permute-start.10 = (f32[4,40,2048]{2,1,0:T(8,128)S(1)}, f32[4,40,2048]{2,1,0:T(8,128)S(1)}, u32[]{:S(2)}, u32[]{:S(2)}) collective-permute-start(f32[4,40,2048]{2,1,0:T(8,128)S(1)} %get-tuple-element.9), channel_id=1, source_target_pairs={{0,1},{1,2},{2,3},{3,4},{4,5},{5,6},{6,7},{7,8},{8,9},{9,10},{10,1... | collective-permute-start | bytes 3932168 | tf_op jit(solution)/shard_map/ppermute | solution.py:28
  177.5 30.8 %collective-permute-start.11 = (f32[4,40,2048]{2,1,0:T(8,128)S(1)}, f32[4,40,2048]{2,1,0:T(8,128)S(1)}, u32[]{:S(2)}, u32[]{:S(2)}) collective-permute-start(f32[4,40,2048]{2,1,0:T(8,128)S(1)} %get-tuple-element.10), channel_id=1, source_target_pairs={{1,0},{2,1},{3,2},{4,3},{5,4},{6,5},{7,6},{8,7},{9,8},{10,9},{11,1... | collective-permute-start | bytes 3932168 | tf_op jit(solution)/shard_map/ppermute | solution.py:30
  213.0 30.6 %collective-permute-start.12 = (f32[4,40,2048]{2,1,0:T(8,128)S(1)}, f32[4,40,2048]{2,1,0:T(8,128)S(1)}, u32[]{:S(2)}, u32[]{:S(2)}) collective-permute-start(f32[4,40,2048]{2,1,0:T(8,128)S(1)} %convolution_bitcast_fusion.3), channel_id=1, source_target_pairs={{0,1},{1,2},{2,3},{3,4},{4,5},{5,6},{6,7},{7,8},{8,9},{9,10},{10,1... | collective-permute-start | bytes 3932168 | tf_op jit(solution)/shard_map/ppermute | solution.py:17
  216.5 29.9 %collective-permute-start.13 = (f32[4,40,2048]{2,1,0:T(8,128)S(1)}, f32[4,40,2048]{2,1,0:T(8,128)S(1)}, u32[]{:S(2)}, u32[]{:S(2)}) collective-permute-start(f32[4,40,2048]{2,1,0:T(8,128)S(1)} %convolution_bitcast_fusion.2), channel_id=1, source_target_pairs={{1,0},{2,1},{3,2},{4,3},{5,4},{6,5},{7,6},{8,7},{9,8},{10,9},{11,1... | collective-permute-start | bytes 3932168 | tf_op jit(solution)/shard_map/ppermute | solution.py:17
  248.4 29.7 %collective-permute-start.14 = (f32[4,40,2048]{2,1,0:T(8,128)S(1)}, f32[4,40,2048]{2,1,0:T(8,128)S(1)}, u32[]{:S(2)}, u32[]{:S(2)}) collective-permute-start(f32[4,40,2048]{2,1,0:T(8,128)S(1)} %get-tuple-element.7), channel_id=1, source_target_pairs={{0,1},{1,2},{2,3},{3,4},{4,5},{5,6},{6,7},{7,8},{8,9},{9,10},{10,1... | collective-permute-start | bytes 3932168 | tf_op jit(solution)/shard_map/ppermute | solution.py:28
  250.3 29.0 %collective-permute-start.15 = (f32[4,40,2048]{2,1,0:T(8,128)S(1)}, f32[4,40,2048]{2,1,0:T(8,128)S(1)}, u32[]{:S(2)}, u32[]{:S(2)}) collective-permute-start(f32[4,40,2048]{2,1,0:T(8,128)S(1)} %get-tuple-element.8), channel_id=1, source_target_pairs={{1,0},{2,1},{3,2},{4,3},{5,4},{6,5},{7,6},{8,7},{9,8},{10,9},{11,1... | collective-permute-start | bytes 3932168 | tf_op jit(solution)/shard_map/ppermute | solution.py:30
  284.0 28.8 %collective-permute-start.16 = (f32[4,40,2048]{2,1,0:T(8,128)S(1)}, f32[4,40,2048]{2,1,0:T(8,128)S(1)}, u32[]{:S(2)}, u32[]{:S(2)}) collective-permute-start(f32[4,40,2048]{2,1,0:T(8,128)S(1)} %convolution_bitcast_fusion.1), channel_id=1, source_target_pairs={{0,1},{1,2},{2,3},{3,4},{4,5},{5,6},{6,7},{7,8},{8,9},{9,10},{10,1... | collective-permute-start | bytes 3932168 | tf_op jit(solution)/shard_map/ppermute | solution.py:17
  287.5 28.0 %collective-permute-start.17 = (f32[4,40,2048]{2,1,0:T(8,128)S(1)}, f32[4,40,2048]{2,1,0:T(8,128)S(1)}, u32[]{:S(2)}, u32[]{:S(2)}) collective-permute-start(f32[4,40,2048]{2,1,0:T(8,128)S(1)} %convolution_bitcast_fusion), channel_id=1, source_target_pairs={{1,0},{2,1},{3,2},{4,3},{5,4},{6,5},{7,6},{8,7},{9,8},{10,9},{11,1... | collective-permute-start | bytes 3932168 | tf_op jit(solution)/shard_map/ppermute | solution.py:17
  314.0 3.1 copy-start.2
  319.0 1.0 copy-start.4
  329.1 252.5 %all-gather.3.cloned.1.call-start = ((), (), s32[]{:S(2)}) async-start(), calls=%async_computation.2 | async-start | bytes 1769472 | tf_op jit(solution)/shard_map/all_gather | solution.py:112
Sparse Core Ops, SparseCore 0:
  329.2 224.2 reduce-scatter.1
  555.5 26.1 all-gather.2
